TPU v7x, 512 devices: a whole 4x4x16 slice. The times are simulated.
512 devices in a mesh: dp: 128 (over z, x, core), mp: 4 (over y).
Axes of the slice: x: 4, y: 4, z: 16, core: 2. Of those that a mesh axis runs over, the one named last changes fastest.
Arguments:
- session_length: int32 [128], P('dp'), may hold values from 1 to 128
- event_owner: int32 [16384, 1], P('dp'), may hold values from 0 to 127; in each aligned block of 128 rows (0 to 127, 128 to 255, ...) at most 2 rows name the same one
- event_row: int32 [16384], P('dp'), may hold values from 0 to 255
- text_rows: bfloat16 [32768, 4096], P('dp', 'mp'), may hold values from -6 to 6
- image_rows: bfloat16 [32768, 4096], P('dp', 'mp'), may hold values from -6 to 6
- price: float32 [32768], P('dp'), may hold values from 0.2 to 5
- price_dir: bfloat16 [4096], P('mp'), may hold values from -4 to 4
- norm_gain: bfloat16 [4096], P('mp'), may hold values from 0.5 to 1.5
- w_query: bfloat16 [4096, 2048], P('dp', 'mp'), may hold values from -1 to 1
- w_key: bfloat16 [4096, 2048], P('dp', 'mp'), may hold values from -1 to 1
- w_value: bfloat16 [4096, 2048], P('dp', 'mp'), may hold values from -0.09375 to 0.09375
- cotangent: bfloat16 [16384, 4096], P('dp', 'mp'), may hold values from -6 to 6
Outputs:
- context: bfloat16 [16384, 2048], P('dp', 'mp')
- text_grad: float32 [32768, 4096], P('dp', 'mp')
- image_grad: float32 [32768, 4096], P('dp', 'mp')
Inputs may be any that keep to these rules, and one draw needn't show every extreme that they name: `event_owner`: among the event slots of one index of dp, no owner is named more than 2 times, a bound that some block reaches.
All inputs are finite; a program needn't handle non-finite values.
Results may differ from a plain program's by a relative error of at most 0.0063.
Values may be sent and summed in bfloat16 or wider, within the bound.
No kernel may reach another device: no remote copies, remote signals or barrier semaphores. Data moves between devices by JAX's collectives and lax.ppermute only.
A program may use at most 64 MiB of HBM per device.

v0:
```python
import math
import jax
import jax.numpy as jnp
from jax import lax
from jax.sharding import PartitionSpec as P

HD = 128
SLOT = 128


def one_hot(rows, columns):
    return (rows[:, None] == columns[None, :]).astype(jnp.bfloat16)


def pick(selector, values):
    return jnp.dot(selector, values, preferred_element_type=jnp.float32)


def attend(query, keys, values, session_length):
    heads_here = query.shape[1] // HD
    shape3 = (SLOT, heads_here, HD)
    scores = jnp.einsum(
        "qhd,khd->hqk",
        query.reshape(shape3),
        keys.reshape(shape3),
        preferred_element_type=jnp.float32,
    ) / math.sqrt(HD)
    position = jnp.arange(SLOT, dtype=jnp.int32)
    live_mask = position < session_length[0]
    allowed = (position[None, :] <= position[:, None])[None] & live_mask[None, None, :]
    scores = jnp.where(allowed, scores, jnp.float32(-1e30))
    row_max = jnp.max(scores, axis=-1, keepdims=True)
    powers = jnp.exp(scores - row_max)
    probs = (powers / jnp.sum(powers, axis=-1, keepdims=True)).astype(jnp.bfloat16)
    context = jnp.einsum(
        "hqk,khd->qhd", probs, values.reshape(shape3), preferred_element_type=jnp.float32
    )
    context = jnp.where(live_mask[:, None, None], context, jnp.float32(0.0))
    return context.reshape(SLOT, heads_here * HD).astype(jnp.bfloat16)


def local(
    session_length,
    event_owner,
    event_row,
    text_rows,
    image_rows,
    price,
    price_dir,
    norm_gain,
    w_query,
    w_key,
    w_value,
    cotangent,
):
    peers = lax.axis_size("dp")
    parts = lax.axis_size("mp")
    mine = lax.axis_index("mp")
    tok_count = event_row.shape[0]
    capacity = 2 * tok_count // peers
    col_width = text_rows.shape[1]
    table_rows = text_rows.shape[0]
    slots = jnp.arange(peers * capacity, dtype=jnp.int32)
    weights = lax.all_gather(
        jnp.concatenate([w_query, w_key, w_value], axis=1), "dp", axis=0, tiled=True
    )
    owner_ids = event_owner[:, 0]
    place = jnp.arange(tok_count, dtype=jnp.int32)
    same = (owner_ids[:, None] == owner_ids[None, :]) & (place[None, :] < place[:, None])
    slot_ids = owner_ids * capacity + jnp.sum(same.astype(jnp.int32), axis=1)
    taken = slots[:, None] == slot_ids[None, :]
    requests = (jnp.sum(jnp.where(taken, event_row[None, :] + 1, 0), axis=1) - 1).reshape(
        peers, capacity
    )
    got_ids = lax.all_to_all(requests, "dp", split_axis=0, concat_axis=0, tiled=True).reshape(-1)
    text_float = text_rows.astype(jnp.float32)
    image_float = image_rows.astype(jnp.float32)
    table = (
        text_float * image_float + price[:, None] * price_dir.astype(jnp.float32)[None, :]
    ).astype(jnp.bfloat16)
    wanted = one_hot(got_ids, jnp.arange(table_rows, dtype=jnp.int32))
    replies = lax.all_to_all(
        pick(wanted, table).astype(jnp.bfloat16).reshape(peers, capacity, col_width),
        "dp",
        split_axis=0,
        concat_axis=0,
        tiled=True,
    ).reshape(peers * capacity, col_width)
    grad_buffer = pick(taken.astype(jnp.bfloat16), cotangent).astype(jnp.bfloat16)
    grad_buffer, replies = lax.optimization_barrier((grad_buffer, replies))
    got_grads = lax.all_to_all(
        grad_buffer.reshape(peers, capacity, col_width),
        "dp",
        split_axis=0,
        concat_axis=0,
        tiled=True,
    ).reshape(peers * capacity, col_width)
    row_sums = pick(wanted.T, got_grads)
    text_grad = row_sums * image_float
    image_grad = row_sums * text_float
    joined = pick(one_hot(slot_ids, slots), replies).astype(jnp.bfloat16)
    turns = [
        (
            joined
            if k == 0
            else lax.ppermute(joined, "mp", [(i, (i + k) % parts) for i in range(parts)])
        )
        for k in range(parts)
    ]
    stacked = jnp.stack(turns)
    features = jnp.concatenate(
        [
            lax.dynamic_index_in_dim(stacked, (mine - s) % parts, 0, keepdims=False)
            for s in range(parts)
        ],
        axis=1,
    ).astype(jnp.float32)
    gain = lax.all_gather(norm_gain, "mp", axis=0, tiled=True).astype(jnp.float32)
    scale = lax.rsqrt(jnp.mean(features * features, axis=1, keepdims=True) + 1e-06)
    normed = (features * scale * gain[None, :]).astype(jnp.bfloat16)
    projected = jnp.dot(normed, weights, preferred_element_type=jnp.float32).astype(jnp.bfloat16)
    width = w_query.shape[1]
    context = attend(
        projected[:, :width],
        projected[:, width : 2 * width],
        projected[:, 2 * width :],
        session_length,
    )
    return (context, text_grad, image_grad)


def solution(mesh):
    return jax.shard_map(
        local,
        mesh=mesh,
        in_specs=(
            P("dp"),
            P("dp", None),
            P("dp"),
            P("dp", "mp"),
            P("dp", "mp"),
            P("dp"),
            P("mp"),
            P("mp"),
            P("dp", "mp"),
            P("dp", "mp"),
            P("dp", "mp"),
            P("dp", "mp"),
        ),
        out_specs=(P("dp", "mp"), P("dp", "mp"), P("dp", "mp")),
        check_vma=False,
    )
```

profile of v0, /device:TPU:1, one launch (start us, length us, event | category | flops | bytes accessed | tf_op | source)
XLA Modules:
  0.0 196.3 jit_solution(1731019495664114980)
XLA Ops:
  7.2 1.5 pad_maximum_fusion.3
  8.7 0.9 convert_reduce_fusion
  9.6 0.7 multiply_add_fusion
  10.4 0.8 sub.24
  11.2 20.4 %all-to-all-start = ((s32[128,1,2]{2,1,0:T(1,128)}), s32[128,1,2]{2,1,0:T(1,128)S(1)}, u32[]{:S(2)}, u32[]{:S(2)}) async-start(s32[128,1,2]{2,1,0:T(1,128)} %bitcast.4), calls=%async_computation | async-start | bytes 131072 | tf_op jit(solution)/shard_map/all_to_all | solution.py:75
  31.6 0.7 convert_element_type.55
  32.3 14.1 %all-to-all-done = s32[128,1,2]{2,1,0:T(1,128)S(1)} async-done(((s32[128,1,2]{2,1,0:T(1,128)}), s32[128,1,2]{2,1,0:T(1,128)S(1)}, u32[]{:S(2)}, u32[]{:S(2)}) %all-to-all-start) | async-done | bytes 1056 | tf_op jit(solution)/shard_map/all_to_all | solution.py:75
  46.4 0.5 broadcast.75
  47.0 0.8 reduce.3
  47.8 0.1 eq.74
  47.9 1.7 convolution_convert_fusion.1
  49.6 1.0 reshape.110
  50.6 5.7 %all-to-all-start.1 = ((bf16[128,2,1024]{2,1,0:T(2,128)(2,1)}), bf16[128,2,1024]{2,1,0:T(2,128)(2,1)S(1)}, u32[]{:S(2)}, u32[]{:S(2)}) async-start(bf16[128,2,1024]{2,1,0:T(2,128)(2,1)} %reshape.110), calls=%async_computation.1 | async-start | bytes 1048576 | tf_op jit(solution)/shard_map/all_to_all | solution.py:82
  56.3 0.3 convolution_convert_fusion.2
  56.6 33.6 %all-to-all-done.1 = bf16[128,2,1024]{2,1,0:T(2,128)(2,1)S(1)} async-done(((bf16[128,2,1024]{2,1,0:T(2,128)(2,1)}), bf16[128,2,1024]{2,1,0:T(2,128)(2,1)S(1)}, u32[]{:S(2)}, u32[]{:S(2)}) %all-to-all-start.1) | async-done | bytes 524320 | tf_op jit(solution)/shard_map/all_to_all | solution.py:82
  90.2 0.2 reshape.111
  90.4 1.0 reshape.115
  91.3 9.5 %all-to-all-start.2 = ((bf16[128,2,1024]{2,1,0:T(2,128)(2,1)}), bf16[128,2,1024]{2,1,0:T(2,128)(2,1)S(1)}, u32[]{:S(2)}, u32[]{:S(2)}) async-start(bf16[128,2,1024]{2,1,0:T(2,128)(2,1)} %reshape.115), calls=%async_computation.2 | async-start | bytes 1048576 | tf_op jit(solution)/shard_map/all_to_all | solution.py:91
  101.6 0.3 convolution_convert_fusion.3
  101.8 3.2 %collective-permute-start = (bf16[128,1024]{1,0:T(8,128)(2,1)S(1)}, bf16[128,1024]{1,0:T(8,128)(2,1)S(1)}, u32[]{:S(2)}, u32[]{:S(2)}) collective-permute-start(bf16[128,1024]{1,0:T(8,128)(2,1)S(1)} %convolution_convert_fusion.3), channel_id=1, source_target_pairs={{0,1},{1,2},{2,3},{3,0},{4,5},{5,6},{6,7},{7,4},{8,9},{9,10},{10,1... | collective-permute-start | bytes 786440 | tf_op jit(solution)/shard_map/ppermute | solution.py:106
  105.0 4.4 %collective-permute-start.1 = (bf16[128,1024]{1,0:T(8,128)(2,1)S(1)}, bf16[128,1024]{1,0:T(8,128)(2,1)S(1)}, u32[]{:S(2)}, u32[]{:S(2)}) collective-permute-start(bf16[128,1024]{1,0:T(8,128)(2,1)S(1)} %convolution_convert_fusion.3), channel_id=1, source_target_pairs={{0,2},{1,3},{2,0},{3,1},{4,6},{5,7},{6,4},{7,5},{8,10},{9,11},{10,... | collective-permute-start | bytes 786440 | tf_op jit(solution)/shard_map/ppermute | solution.py:106
  109.4 3.0 %collective-permute-start.2 = (bf16[128,1024]{1,0:T(8,128)(2,1)S(1)}, bf16[128,1024]{1,0:T(8,128)(2,1)S(1)}, u32[]{:S(2)}, u32[]{:S(2)}) collective-permute-start(bf16[128,1024]{1,0:T(8,128)(2,1)S(1)} %convolution_convert_fusion.3), channel_id=1, source_target_pairs={{0,3},{1,0},{2,1},{3,2},{4,7},{5,4},{6,5},{7,6},{8,11},{9,8},{10,9... | collective-permute-start | bytes 786440 | tf_op jit(solution)/shard_map/ppermute | solution.py:106
  112.5 13.0 %all_gather.6 = bf16[4096]{0:T(1024)(128)(2,1)S(1)} all-gather(bf16[1024]{0:T(1024)(128)(2,1)S(1)} %copy-done.3), channel_id=1, replica_groups=mesh['dp'=128,'mp'=4] {'mp'}, dimensions={0}, use_global_device_ids=true | all-gather | bytes 10240 | tf_op jit(solution)/shard_map/all_gather | solution.py:118
  126.0 0.3 fusion.1
  126.3 7.7 %all-to-all-done.2 = bf16[128,2,1024]{2,1,0:T(2,128)(2,1)S(1)} async-done(((bf16[128,2,1024]{2,1,0:T(2,128)(2,1)}), bf16[128,2,1024]{2,1,0:T(2,128)(2,1)S(1)}, u32[]{:S(2)}, u32[]{:S(2)}) %all-to-all-start.2) | async-done | bytes 524320 | tf_op jit(solution)/shard_map/all_to_all | solution.py:91
  134.0 0.2 reshape.116
  134.3 1.7 convert_multiply_fusion.4
  136.0 45.6 %all-gather.2.cloned.1.call-done = bf16[4096,1536]{1,0:T(8,128)(2,1)} async-done(((bf16[32,1536]{1,0:T(8,128)(2,1)}), bf16[4096,1536]{1,0:T(8,128)(2,1)}) %all-gather.2.cloned.1.call-update) | async-done | bytes 12582928 | tf_op jit(solution)/shard_map/all_gather | solution.py:64
  181.6 6.4 %convolution_convert_fusion = bf16[128,1536]{1,0:T(8,128)(2,1)S(1)} fusion(bf16[4096,1536]{1,0:T(8,128)(2,1)} %all-gather.2.cloned.1.call-done, f32[4096]{0:T(1024)S(1)} %convert_element_type.60, f32[128]{0:T(128)S(1)} %add_rsqrt_fusion, bf16[128,1024]{1,0:T(8,128)(2,1)S(1)} %get-tuple-element.22, bf16[128,1024]{1,0:T(8,128)(2,1)S(1)} %get-tuple-element.23, ...), kind=kOutput, calls=%fused_computation.3 | convolution fusion | flops 1616576512 | bytes 14041600 | tf_op jit(solution)/shard_map/dot_general | solution.py:121
  188.0 0.2 fusion.5
  188.4 0.2 fusion.7
  188.7 0.8 copy.36
  (27 shorter events, 0.8 us)
Async XLA Ops:
  7.2 49.1 %copy-start = (bf16[128,1024]{1,0:T(8,128)(2,1)S(1)}, bf16[128,1024]{1,0:T(8,128)(2,1)}, u32[]{:S(2)}) copy-start(bf16[128,1024]{1,0:T(8,128)(2,1)} %param.23) | copy-start | bytes 786436
  7.2 174.4 %all-gather.2.cloned.1.call-start = ((), (), s32[]{:S(2)}) async-start(), calls=%async_computation.3 | async-start | bytes 12681216 | tf_op jit(solution)/shard_map/all_gather | solution.py:64
  11.2 35.2 %all-to-all-start = ((s32[128,1,2]{2,1,0:T(1,128)}), s32[128,1,2]{2,1,0:T(1,128)S(1)}, u32[]{:S(2)}, u32[]{:S(2)}) async-start(s32[128,1,2]{2,1,0:T(1,128)} %bitcast.4), calls=%async_computation | async-start | bytes 131072 | tf_op jit(solution)/shard_map/all_to_all | solution.py:75
  50.6 39.6 %all-to-all-start.1 = ((bf16[128,2,1024]{2,1,0:T(2,128)(2,1)}), bf16[128,2,1024]{2,1,0:T(2,128)(2,1)S(1)}, u32[]{:S(2)}, u32[]{:S(2)}) async-start(bf16[128,2,1024]{2,1,0:T(2,128)(2,1)} %reshape.110), calls=%async_computation.1 | async-start | bytes 1048576 | tf_op jit(solution)/shard_map/all_to_all | solution.py:82
  56.3 45.3 %copy-start.4 = (s32[128,1]{0,1:T(1,128)S(1)}, s32[128,1]{0,1:T(1,128)}, u32[]{:S(2)}) copy-start(s32[128,1]{0,1:T(1,128)} %param.13) | copy-start | bytes 1540
  56.6 56.0 %copy-start.3 = (bf16[1024]{0:T(1024)(128)(2,1)S(1)}, bf16[1024]{0:T(1024)(128)(2,1)}, u32[]{:S(2)}) copy-start(bf16[1024]{0:T(1024)(128)(2,1)} %param.19) | copy-start | bytes 6148
  91.3 42.7 %all-to-all-start.2 = ((bf16[128,2,1024]{2,1,0:T(2,128)(2,1)}), bf16[128,2,1024]{2,1,0:T(2,128)(2,1)S(1)}, u32[]{:S(2)}, u32[]{:S(2)}) async-start(bf16[128,2,1024]{2,1,0:T(2,128)(2,1)} %reshape.115), calls=%async_computation.2 | async-start | bytes 1048576 | tf_op jit(solution)/shard_map/all_to_all | solution.py:91
  101.8 23.9 %collective-permute-start = (bf16[128,1024]{1,0:T(8,128)(2,1)S(1)}, bf16[128,1024]{1,0:T(8,128)(2,1)S(1)}, u32[]{:S(2)}, u32[]{:S(2)}) collective-permute-start(bf16[128,1024]{1,0:T(8,128)(2,1)S(1)} %convolution_convert_fusion.3), channel_id=1, source_target_pairs={{0,1},{1,2},{2,3},{3,0},{4,5},{5,6},{6,7},{7,4},{8,9},{9,10},{10,1... | collective-permute-start | bytes 786440 | tf_op jit(solution)/shard_map/ppermute | solution.py:106
  105.0 20.7 %collective-permute-start.1 = (bf16[128,1024]{1,0:T(8,128)(2,1)S(1)}, bf16[128,1024]{1,0:T(8,128)(2,1)S(1)}, u32[]{:S(2)}, u32[]{:S(2)}) collective-permute-start(bf16[128,1024]{1,0:T(8,128)(2,1)S(1)} %convolution_convert_fusion.3), channel_id=1, source_target_pairs={{0,2},{1,3},{2,0},{3,1},{4,6},{5,7},{6,4},{7,5},{8,10},{9,11},{10,... | collective-permute-start | bytes 786440 | tf_op jit(solution)/shard_map/ppermute | solution.py:106
  109.4 16.3 %collective-permute-start.2 = (bf16[128,1024]{1,0:T(8,128)(2,1)S(1)}, bf16[128,1024]{1,0:T(8,128)(2,1)S(1)}, u32[]{:S(2)}, u32[]{:S(2)}) collective-permute-start(bf16[128,1024]{1,0:T(8,128)(2,1)S(1)} %convolution_convert_fusion.3), channel_id=1, source_target_pairs={{0,3},{1,0},{2,1},{3,2},{4,7},{5,4},{6,5},{7,6},{8,11},{9,8},{10,9... | collective-permute-start | bytes 786440 | tf_op jit(solution)/shard_map/ppermute | solution.py:106
  125.9 8.4 %copy-start.1 = (bf16[256,1024]{1,0:T(8,128)(2,1)S(1)}, bf16[256,1024]{1,0:T(8,128)(2,1)}, u32[]{:S(2)}) copy-start(bf16[256,1024]{1,0:T(8,128)(2,1)} %param.16) | copy-start | bytes 1572868
  125.9 8.4 %copy-start.2 = (bf16[256,1024]{1,0:T(8,128)(2,1)S(1)}, bf16[256,1024]{1,0:T(8,128)(2,1)}, u32[]{:S(2)}) copy-start(bf16[256,1024]{1,0:T(8,128)(2,1)} %param.15) | copy-start | bytes 1572868
Sparse Core Ops, SparseCore 0:
  11.7 169.7 all-gather.1
where the time goes:
time: 197 us; the launch traced here: 196 us
  waiting for transfers between devices  101 us (51%)
  starting transfers between devices  46.2 us (23%)
  between operations  15.1 us (8%)
  blocking collectives  13 us (7%)
  matrix products  10.8 us (5%)
  other arithmetic  5.29 us (3%)
  local copies, waits for them, and re-layouts  4.84 us (2%)
    all_gather x1, waiting for transfers between devices, local(): lax.all_gather(jnp.concatenate([w_query, w_key, w_value], axis=1), 'dp',...  45.6 us
    all_to_all x1, waiting for transfers between devices, local(): lax.all_to_all(pick(wanted, table).astype(jnp.bfloat16).reshape(peers, ca...  33.6 us
    all_to_all x1, starting transfers between devices, local(): lax.all_to_all(requests, 'dp', split_axis=0, concat_axis=0, tiled=True)  20.4 us
    all_to_all x1, waiting for transfers between devices, local(): lax.all_to_all(requests, 'dp', split_axis=0, concat_axis=0, tiled=True)  14.1 us
    all_gather x1, blocking collectives, local(): lax.all_gather(norm_gain, 'mp', axis=0, tiled=True).astype(jnp.float32)  13 us
    ppermute x3, starting transfers between devices, local(): lax.ppermute(joined, 'mp', [(i, (i + k) % parts) for i in range(parts)])  10.6 us
    all_to_all x1, starting transfers between devices, local(): lax.all_to_all(grad_buffer.reshape(peers, capacity, col_width), 'dp', spl...  9.53 us
    all_to_all x1, waiting for transfers between devices, local(): lax.all_to_all(grad_buffer.reshape(peers, capacity, col_width), 'dp', spl...  7.74 us
  transfers between devices with their start and end apart: 7, of which 4 were waited for; matrix products, arithmetic and copies ran while one was open for 6% of the time, Pallas kernels for 0%

commit v1 on v0

--- a/solution.py
+++ b/solution.py
@@ -6,6 +6,13 @@
 
 HD = 128
 SLOT = 128
+
+
+def gather_over(x, mesh_axis, dim):
+    size = lax.axis_size(mesh_axis)
+    shards = jnp.stack([x for _ in range(size)])
+    shards = lax.all_to_all(shards, mesh_axis, split_axis=0, concat_axis=0)
+    return jnp.concatenate(shards, axis=dim)
 
 
 def one_hot(rows, columns):
@@ -115,7 +122,7 @@
         ],
         axis=1,
     ).astype(jnp.float32)
-    gain = lax.all_gather(norm_gain, "mp", axis=0, tiled=True).astype(jnp.float32)
+    gain = gather_over(norm_gain, "mp", 0).astype(jnp.float32)
     scale = lax.rsqrt(jnp.mean(features * features, axis=1, keepdims=True) + 1e-06)
     normed = (features * scale * gain[None, :]).astype(jnp.bfloat16)
     projected = jnp.dot(normed, weights, preferred_element_type=jnp.float32).astype(jnp.bfloat16)

time: 197 us -> 203 us (1.030)
  waiting for transfers between devices: 101 us -> 115 us
  blocking collectives: 13 us -> 0 us
  starting transfers between devices: 46.2 us -> 49.9 us
    all_gather x1 -> x0, blocking collectives: 13 us -> none  [local(): lax.all_gather(norm_gain, 'mp', axis=0, tiled=True).astype(jnp.float32)]
    all_to_all x1, waiting for transfers between devices: 7.74 us -> 17.3 us  [local(): lax.all_to_all(grad_buffer.reshape(peers, capacity, col_width), 'dp', spl...]
    ppermute x3, waiting for transfers between devices: 0.01 us -> 9.33 us  [local(): lax.ppermute(joined, 'mp', [(i, (i + k) % parts) for i in range(parts)])]
    all_gather x1, waiting for transfers between devices: 45.6 us -> 39.5 us  [local(): lax.all_gather(jnp.concatenate([w_query, w_key, w_value], axis=1), 'dp',...]
    all_to_all x0 -> x1, starting transfers between devices: none -> 4.03 us  [gather_over(): shards = lax.all_to_all(shards, mesh_axis, split_axis=0, concat_axis=0)]
    all_to_all x0 -> x1, waiting for transfers between devices: none -> 2.67 us  [gather_over(): shards = lax.all_to_all(shards, mesh_axis, split_axis=0, concat_axis=0)]
  transfers between devices with their start and end apart: 7 -> 8, of which waited for: 4 -> 8; matrix products, arithmetic and copies ran while one was open for 6% -> 7% of each run, Pallas kernels for 0% -> 0%
where the time goes in v1:
time: 203 us
  waiting for transfers between devices  115 us (57%)
  starting transfers between devices  49.9 us (25%)
  between operations  15 us (7%)
  matrix products  10.8 us (5%)
  other arithmetic  5.99 us (3%)
  local copies, waits for them, and re-layouts  5.98 us (3%)
    all_gather x1, waiting for transfers between devices, local(): lax.all_gather(jnp.concatenate([w_query, w_key, w_value], axis=1), 'dp',...  39.5 us
    all_to_all x1, waiting for transfers between devices, local(): lax.all_to_all(pick(wanted, table).astype(jnp.bfloat16).reshape(peers, ca...  32.2 us
    all_to_all x1, starting transfers between devices, local(): lax.all_to_all(requests, 'dp', split_axis=0, concat_axis=0, tiled=True)  20.4 us
    all_to_all x1, waiting for transfers between devices, local(): lax.all_to_all(grad_buffer.reshape(peers, capacity, col_width), 'dp', spl...  17.3 us
    all_to_all x1, waiting for transfers between devices, local(): lax.all_to_all(requests, 'dp', split_axis=0, concat_axis=0, tiled=True)  14.1 us
    all_to_all x1, starting transfers between devices, local(): lax.all_to_all(grad_buffer.reshape(peers, capacity, col_width), 'dp', spl...  10.9 us
    ppermute x3, waiting for transfers between devices, local(): lax.ppermute(joined, 'mp', [(i, (i + k) % parts) for i in range(parts)])  9.33 us
    ppermute x3, starting transfers between devices, local(): lax.ppermute(joined, 'mp', [(i, (i + k) % parts) for i in range(parts)])  8.84 us
  transfers between devices with their start and end apart: 8, of which 8 were waited for; matrix products, arithmetic and copies ran while one was open for 7% of the time, Pallas kernels for 0%

profile of v1, /device:TPU:1, one launch (start us, length us, event | category | flops | bytes accessed | tf_op | source)
XLA Modules:
  0.0 202.9 jit_solution(6667498948460766797)
XLA Ops:
  7.2 1.5 pad_maximum_fusion.3
  8.7 0.9 convert_reduce_fusion
  9.6 0.7 multiply_add_fusion
  10.4 0.8 sub.24
  11.2 20.4 %all-to-all-start = ((s32[128,1,2]{2,1,0:T(1,128)}), s32[128,1,2]{2,1,0:T(1,128)S(1)}, u32[]{:S(2)}, u32[]{:S(2)}) async-start(s32[128,1,2]{2,1,0:T(1,128)} %bitcast.4), calls=%async_computation | async-start | bytes 131072 | tf_op jit(solution)/shard_map/all_to_all | solution.py:82
  31.6 0.7 convert_element_type.62
  32.3 14.1 %all-to-all-done = s32[128,1,2]{2,1,0:T(1,128)S(1)} async-done(((s32[128,1,2]{2,1,0:T(1,128)}), s32[128,1,2]{2,1,0:T(1,128)S(1)}, u32[]{:S(2)}, u32[]{:S(2)}) %all-to-all-start) | async-done | bytes 1056 | tf_op jit(solution)/shard_map/all_to_all | solution.py:82
  46.4 0.5 broadcast.78
  47.0 0.8 reduce.3
  47.9 1.7 convolution_convert_fusion.1
  49.6 1.0 reshape.125
  50.6 5.7 %all-to-all-start.1 = ((bf16[128,2,1024]{2,1,0:T(2,128)(2,1)}), bf16[128,2,1024]{2,1,0:T(2,128)(2,1)S(1)}, u32[]{:S(2)}, u32[]{:S(2)}) async-start(bf16[128,2,1024]{2,1,0:T(2,128)(2,1)} %reshape.125), calls=%async_computation.1 | async-start | bytes 1048576 | tf_op jit(solution)/shard_map/all_to_all | solution.py:89
  56.3 0.5 broadcast.79
  56.8 0.7 reduce.4
  57.5 0.6 reshape.142
  58.1 32.2 %all-to-all-done.1 = bf16[128,2,1024]{2,1,0:T(2,128)(2,1)S(1)} async-done(((bf16[128,2,1024]{2,1,0:T(2,128)(2,1)}), bf16[128,2,1024]{2,1,0:T(2,128)(2,1)S(1)}, u32[]{:S(2)}, u32[]{:S(2)}) %all-to-all-start.1) | async-done | bytes 524320 | tf_op jit(solution)/shard_map/all_to_all | solution.py:89
  90.3 4.0 %all-to-all-start.2 = ((bf16[4,2,512]{2,1,0:T(2,128)(2,1)}), bf16[4,2,512]{2,1,0:T(2,128)(2,1)S(1)}, u32[]{:S(2)}, u32[]{:S(2)}) async-start(bf16[4,2,512]{2,1,0:T(2,128)(2,1)} %reshape.142), calls=%async_computation.2 | async-start | bytes 16384 | tf_op jit(solution)/shard_map/all_to_all | solution.py:14
  94.8 1.0 reshape.130
  95.8 2.7 %all-to-all-done.2 = bf16[4,2,512]{2,1,0:T(2,128)(2,1)S(1)} async-done(((bf16[4,2,512]{2,1,0:T(2,128)(2,1)}), bf16[4,2,512]{2,1,0:T(2,128)(2,1)S(1)}, u32[]{:S(2)}, u32[]{:S(2)}) %all-to-all-start.2) | async-done | bytes 8224 | tf_op jit(solution)/shard_map/all_to_all | solution.py:14
  98.5 10.9 %all-to-all-start.3 = ((bf16[128,2,1024]{2,1,0:T(2,128)(2,1)}), bf16[128,2,1024]{2,1,0:T(2,128)(2,1)S(1)}, u32[]{:S(2)}, u32[]{:S(2)}) async-start(bf16[128,2,1024]{2,1,0:T(2,128)(2,1)} %reshape.130), calls=%async_computation.3 | async-start | bytes 1048576 | tf_op jit(solution)/shard_map/all_to_all | solution.py:98
  110.3 2.2 %collective-permute-start = (bf16[128,1024]{1,0:T(8,128)(2,1)S(1)}, bf16[128,1024]{1,0:T(8,128)(2,1)S(1)}, u32[]{:S(2)}, u32[]{:S(2)}) collective-permute-start(bf16[128,1024]{1,0:T(8,128)(2,1)S(1)} %convolution_convert_fusion.3), channel_id=1, source_target_pairs={{0,1},{1,2},{2,3},{3,0},{4,5},{5,6},{6,7},{7,4},{8,9},{9,10},{10,1... | collective-permute-start | bytes 786440 | tf_op jit(solution)/shard_map/ppermute | solution.py:113
  112.5 3.7 %collective-permute-start.1 = (bf16[128,1024]{1,0:T(8,128)(2,1)S(1)}, bf16[128,1024]{1,0:T(8,128)(2,1)S(1)}, u32[]{:S(2)}, u32[]{:S(2)}) collective-permute-start(bf16[128,1024]{1,0:T(8,128)(2,1)S(1)} %convolution_convert_fusion.3), channel_id=1, source_target_pairs={{0,2},{1,3},{2,0},{3,1},{4,6},{5,7},{6,4},{7,5},{8,10},{9,11},{10,... | collective-permute-start | bytes 786440 | tf_op jit(solution)/shard_map/ppermute | solution.py:113
  116.2 3.0 %collective-permute-start.2 = (bf16[128,1024]{1,0:T(8,128)(2,1)S(1)}, bf16[128,1024]{1,0:T(8,128)(2,1)S(1)}, u32[]{:S(2)}, u32[]{:S(2)}) collective-permute-start(bf16[128,1024]{1,0:T(8,128)(2,1)S(1)} %convolution_convert_fusion.3), channel_id=1, source_target_pairs={{0,3},{1,0},{2,1},{3,2},{4,7},{5,4},{6,5},{7,6},{8,11},{9,8},{10,9... | collective-permute-start | bytes 786440 | tf_op jit(solution)/shard_map/ppermute | solution.py:113
  119.4 1.6 collective-permute-done
  121.0 4.3 %collective-permute-done.1 = bf16[128,1024]{1,0:T(8,128)(2,1)S(1)} collective-permute-done((bf16[128,1024]{1,0:T(8,128)(2,1)S(1)}, bf16[128,1024]{1,0:T(8,128)(2,1)S(1)}, u32[]{:S(2)}, u32[]{:S(2)}) %collective-permute-start.1) | collective-permute-done | bytes 262176 | tf_op jit(solution)/shard_map/ppermute | solution.py:113
  125.4 3.4 %collective-permute-done.2 = bf16[128,1024]{1,0:T(8,128)(2,1)S(1)} collective-permute-done((bf16[128,1024]{1,0:T(8,128)(2,1)S(1)}, bf16[128,1024]{1,0:T(8,128)(2,1)S(1)}, u32[]{:S(2)}, u32[]{:S(2)}) %collective-permute-start.2) | collective-permute-done | bytes 262176 | tf_op jit(solution)/shard_map/ppermute | solution.py:113
  129.0 0.3 fusion.1
  129.3 17.3 %all-to-all-done.3 = bf16[128,2,1024]{2,1,0:T(2,128)(2,1)S(1)} async-done(((bf16[128,2,1024]{2,1,0:T(2,128)(2,1)}), bf16[128,2,1024]{2,1,0:T(2,128)(2,1)S(1)}, u32[]{:S(2)}, u32[]{:S(2)}) %all-to-all-start.3) | async-done | bytes 524320 | tf_op jit(solution)/shard_map/all_to_all | solution.py:98
  146.8 1.7 convert_multiply_fusion.4
  148.6 39.5 %all-gather.2.cloned.1.call-done = bf16[4096,1536]{1,0:T(8,128)(2,1)} async-done(((bf16[32,1536]{1,0:T(8,128)(2,1)}), bf16[4096,1536]{1,0:T(8,128)(2,1)}) %all-gather.2.cloned.1.call-update) | async-done | bytes 12582928 | tf_op jit(solution)/shard_map/all_gather | solution.py:71
  188.1 6.4 %convolution_convert_fusion = bf16[128,1536]{1,0:T(8,128)(2,1)S(1)} fusion(bf16[4096,1536]{1,0:T(8,128)(2,1)} %all-gather.2.cloned.1.call-done, f32[4096]{0:T(1024)S(1)} %bitcast.51, f32[128]{0:T(128)S(1)} %add_rsqrt_fusion, bf16[128,1024]{1,0:T(8,128)(2,1)S(1)} %get-tuple-element.22, bf16[128,1024]{1,0:T(8,128)(2,1)S(1)} %get-tuple-element.23, ...), kind=kOutput, calls=%fused_computation.3 | convolution fusion | flops 1616576512 | bytes 14041600 | tf_op jit(solution)/shard_map/dot_general | solution.py:128
  195.2 0.8 copy.36
  (33 shorter events, 2.3 us)
Async XLA Ops:
  7.2 87.2 %copy-start = (bf16[128,1024]{1,0:T(8,128)(2,1)S(1)}, bf16[128,1024]{1,0:T(8,128)(2,1)}, u32[]{:S(2)}) copy-start(bf16[128,1024]{1,0:T(8,128)(2,1)} %param.23) | copy-start | bytes 786436
  7.2 180.9 %all-gather.2.cloned.1.call-start = ((), (), s32[]{:S(2)}) async-start(), calls=%async_computation.4 | async-start | bytes 12681216 | tf_op jit(solution)/shard_map/all_gather | solution.py:71
  10.4 45.8 %copy-start.3 = (bf16[1024]{0:T(1024)(128)(2,1)S(1)}, bf16[1024]{0:T(1024)(128)(2,1)}, u32[]{:S(2)}) copy-start(bf16[1024]{0:T(1024)(128)(2,1)} %param.19) | copy-start | bytes 6148
  11.2 35.2 %all-to-all-start = ((s32[128,1,2]{2,1,0:T(1,128)}), s32[128,1,2]{2,1,0:T(1,128)S(1)}, u32[]{:S(2)}, u32[]{:S(2)}) async-start(s32[128,1,2]{2,1,0:T(1,128)} %bitcast.4), calls=%async_computation | async-start | bytes 131072 | tf_op jit(solution)/shard_map/all_to_all | solution.py:82
  50.6 39.7 %all-to-all-start.1 = ((bf16[128,2,1024]{2,1,0:T(2,128)(2,1)}), bf16[128,2,1024]{2,1,0:T(2,128)(2,1)S(1)}, u32[]{:S(2)}, u32[]{:S(2)}) async-start(bf16[128,2,1024]{2,1,0:T(2,128)(2,1)} %reshape.125), calls=%async_computation.1 | async-start | bytes 1048576 | tf_op jit(solution)/shard_map/all_to_all | solution.py:89
  56.3 53.8 %copy-start.4 = (s32[128,1]{0,1:T(1,128)S(1)}, s32[128,1]{0,1:T(1,128)}, u32[]{:S(2)}) copy-start(s32[128,1]{0,1:T(1,128)} %param.13) | copy-start | bytes 1540
  90.3 8.2 %all-to-all-start.2 = ((bf16[4,2,512]{2,1,0:T(2,128)(2,1)}), bf16[4,2,512]{2,1,0:T(2,128)(2,1)S(1)}, u32[]{:S(2)}, u32[]{:S(2)}) async-start(bf16[4,2,512]{2,1,0:T(2,128)(2,1)} %reshape.142), calls=%async_computation.2 | async-start | bytes 16384 | tf_op jit(solution)/shard_map/all_to_all | solution.py:14
  98.5 48.1 %all-to-all-start.3 = ((bf16[128,2,1024]{2,1,0:T(2,128)(2,1)}), bf16[128,2,1024]{2,1,0:T(2,128)(2,1)S(1)}, u32[]{:S(2)}, u32[]{:S(2)}) async-start(bf16[128,2,1024]{2,1,0:T(2,128)(2,1)} %reshape.130), calls=%async_computation.3 | async-start | bytes 1048576 | tf_op jit(solution)/shard_map/all_to_all | solution.py:98
  110.3 10.7 %collective-permute-start = (bf16[128,1024]{1,0:T(8,128)(2,1)S(1)}, bf16[128,1024]{1,0:T(8,128)(2,1)S(1)}, u32[]{:S(2)}, u32[]{:S(2)}) collective-permute-start(bf16[128,1024]{1,0:T(8,128)(2,1)S(1)} %convolution_convert_fusion.3), channel_id=1, source_target_pairs={{0,1},{1,2},{2,3},{3,0},{4,5},{5,6},{6,7},{7,4},{8,9},{9,10},{10,1... | collective-permute-start | bytes 786440 | tf_op jit(solution)/shard_map/ppermute | solution.py:113
  112.5 12.9 %collective-permute-start.1 = (bf16[128,1024]{1,0:T(8,128)(2,1)S(1)}, bf16[128,1024]{1,0:T(8,128)(2,1)S(1)}, u32[]{:S(2)}, u32[]{:S(2)}) collective-permute-start(bf16[128,1024]{1,0:T(8,128)(2,1)S(1)} %convolution_convert_fusion.3), channel_id=1, source_target_pairs={{0,2},{1,3},{2,0},{3,1},{4,6},{5,7},{6,4},{7,5},{8,10},{9,11},{10,... | collective-permute-start | bytes 786440 | tf_op jit(solution)/shard_map/ppermute | solution.py:113
  116.2 12.5 %collective-permute-start.2 = (bf16[128,1024]{1,0:T(8,128)(2,1)S(1)}, bf16[128,1024]{1,0:T(8,128)(2,1)S(1)}, u32[]{:S(2)}, u32[]{:S(2)}) collective-permute-start(bf16[128,1024]{1,0:T(8,128)(2,1)S(1)} %convolution_convert_fusion.3), channel_id=1, source_target_pairs={{0,3},{1,0},{2,1},{3,2},{4,7},{5,4},{6,5},{7,6},{8,11},{9,8},{10,9... | collective-permute-start | bytes 786440 | tf_op jit(solution)/shard_map/ppermute | solution.py:113
  128.9 17.9 %copy-start.1 = (bf16[256,1024]{1,0:T(8,128)(2,1)S(1)}, bf16[256,1024]{1,0:T(8,128)(2,1)}, u32[]{:S(2)}) copy-start(bf16[256,1024]{1,0:T(8,128)(2,1)} %param.16) | copy-start | bytes 1572868
  128.9 17.9 %copy-start.2 = (bf16[256,1024]{1,0:T(8,128)(2,1)S(1)}, bf16[256,1024]{1,0:T(8,128)(2,1)}, u32[]{:S(2)}) copy-start(bf16[256,1024]{1,0:T(8,128)(2,1)} %param.15) | copy-start | bytes 1572868
Sparse Core Ops, SparseCore 0:
  11.7 176.3 all-gather.1
